TPU v7x, 32 devices: a whole 2x2x4 slice. The times are simulated.
32 devices in a mesh: img: 2 (over y), cls: 4 (over z), emb: 4 (over x, core).
Axes of the slice: x: 2, y: 2, z: 4, core: 2. Of those that a mesh axis runs over, the one named last changes fastest.
Arguments:
- regions: bfloat16 [2048, 1024], P('img', 'emb'), may hold values from -8 to 8
- table: bfloat16 [21504, 1024], P('cls', 'emb'), may hold values from -1 to 1
- shift: float32 [2048], P('img'), may hold values from -0.5 to 0.1
- scale: float32 [2048], P('img'), may hold values from 2 to 20
- labels: int32 [2048], P('img'), may hold values from -1 to 21503, as said below
- valid: int32 [4, 21504], P('img', 'cls'), may hold values 0 or 1
Outputs:
- loss: float32 [], replicated
- region_grad: bfloat16 [2048, 1024], P('img', 'emb')
- table_grad: bfloat16 [21504, 1024], P('cls', 'emb')
Inputs may be any that keep to these rules, and one draw needn't show every extreme that they name: `labels`: -1 marks background; the first region of every image is foreground.
All inputs are finite; a program needn't handle non-finite values. No bound on the sum of `valid` on one device may be relied on, other than what follows from the above.
Results may differ from a plain program's by a relative error of at most 0.0034.
Values may be sent and summed in bfloat16 or wider, within the bound.
A program may use at most 64 MiB of HBM per device.

v0:
```python
import jax
import jax.numpy as jnp
from jax import lax
from jax.sharding import PartitionSpec as P

CLASSES = 21504
REG_IMG = 512


def focal(logit, target):
    prob = jax.nn.sigmoid(logit)
    return -0.25 * target * (1.0 - prob) ** 2 * jax.nn.log_sigmoid(logit) - 0.75 * (
        1.0 - target
    ) * prob**2 * jax.nn.log_sigmoid(-logit)


def shards(regions, table, shift, scale, labels, valid):
    rows = regions.shape[0]
    class_dev = table.shape[0]
    parts = lax.axis_size("emb")
    quarter = rows // parts
    start = lax.axis_index("emb") * quarter
    block = regions.astype(jnp.float32)
    squares = lax.psum(jnp.sum(block * block, axis=1), "emb")
    local_count = jnp.sum((labels >= 0).astype(jnp.float32))
    count = lax.psum(local_count, "img")
    inv = lax.rsqrt(squares + 1e-06)
    unit = block * inv[:, None]
    unit_b = unit.astype(jnp.bfloat16)
    unit_rows = lax.all_to_all(unit_b, "emb", split_axis=0, concat_axis=1, tiled=True)
    cosine = lax.dot_general(
        unit_rows,
        lax.all_gather(table, "emb", axis=1, tiled=True),
        (((1,), (1,)), ((), ())),
        preferred_element_type=jnp.float32,
    )
    shift_q = lax.dynamic_slice_in_dim(shift, start, quarter, 0)
    scale_q = lax.dynamic_slice_in_dim(scale, start, quarter, 0)
    label_q = lax.dynamic_slice_in_dim(labels, start, quarter, 0)
    image_ids = (start + jnp.arange(quarter, dtype=jnp.int32)) // REG_IMG
    onehot = (image_ids[:, None] == jnp.arange(valid.shape[0], dtype=jnp.int32)[None, :]).astype(
        jnp.float32
    )
    mask = jnp.dot(onehot, valid.astype(jnp.float32), preferred_element_type=jnp.float32)
    class_ids = lax.axis_index("cls") * class_dev + jnp.arange(class_dev, dtype=jnp.int32)
    logit = (cosine + shift_q[:, None]) * scale_q[:, None]
    target = (label_q[:, None] == class_ids[None, :]).astype(jnp.float32)
    term, pullback = jax.vjp(lambda value: focal(value, target), logit)
    dlogit = pullback(jnp.ones_like(term))[0]
    total = lax.psum(jnp.sum(term * mask), ("img", "cls", "emb"))
    factor = rows * lax.axis_size("img") / count
    dscore = (dlogit * mask * scale_q[:, None] * factor).astype(jnp.bfloat16)
    piece = lax.all_gather(dscore, "emb", axis=0, tiled=True)
    dunit_piece = jnp.dot(piece, table, preferred_element_type=jnp.float32)
    table_acc = lax.dot_general(
        piece, unit_b, (((0,), (0,)), ((), ())), preferred_element_type=jnp.float32
    )
    dunit = lax.psum(dunit_piece, "cls")
    radial = lax.psum(jnp.sum(unit * dunit, axis=1), "emb")
    region_grad = (inv[:, None] * (dunit - unit * radial[:, None])).astype(jnp.bfloat16)
    table_grad = lax.psum(table_acc, "img").astype(jnp.bfloat16)
    loss = total / count / CLASSES
    return (loss, region_grad, table_grad)


def solution(mesh):
    placed = (P("img", "emb"), P("cls", "emb"), P("img"), P("img"), P("img"), P("img", "cls"))
    return jax.shard_map(
        shards,
        mesh=mesh,
        in_specs=placed,
        out_specs=(P(), P("img", "emb"), P("cls", "emb")),
        check_vma=False,
    )
```

profile of v0, /device:TPU:0, one launch (start us, length us, event | category | flops | bytes accessed | tf_op | source)
XLA Modules:
  0.0 357.9 jit_solution(13751728279272978331)
XLA Ops:
  7.2 0.0 copy-start.2
  7.2 0.0 all-gather.3.cloned.1.call-start
  7.2 0.7 all-gather.3.cloned.1.call-update
  7.9 1.3 fusion.33
  9.2 8.4 %psum.42 = f32[1024]{0:T(1024)S(1)} all-reduce(f32[1024]{0:T(1024)S(1)} %fusion.33), channel_id=1, replica_groups=mesh['img'=2,'cls'=4,'emb'=4] {'emb'}, use_global_device_ids=true, to_apply=%region_1.0 | all-reduce | flops 1024 | bytes 8192 | tf_op jit(solution)/shard_map/psum | solution.py:24
  17.6 1.3 fusion.28
  18.9 1.0 copy.9
  19.9 3.5 all-to-all-start
  23.4 0.0 all-gather.5.cloned.1.call-start
  23.5 0.0 copy-done.2
  23.5 0.6 convert_reduce_fusion
  24.1 5.5 %psum.44 = f32[]{:T(128)} all-reduce(f32[]{:T(128)} %convert_reduce_fusion), channel_id=1, replica_groups=mesh['img'=2,'cls'=4,'emb'=4] {'img'}, use_global_device_ids=true, to_apply=%region_5.7 | all-reduce | flops 1 | bytes 8 | tf_op jit(solution)/shard_map/psum | solution.py:26
  29.6 0.1 dynamic_slice.9
  29.7 0.8 dynamic_slice.11
  30.5 0.8 dynamic_slice.10
  31.9 6.3 %all-to-all-done = bf16[4,256,256]{1,2,0:T(8,128)(2,1)S(1)} async-done(((bf16[4,256,256]{1,2,0:T(8,128)(2,1)}), bf16[4,256,256]{1,2,0:T(8,128)(2,1)S(1)}, u32[]{:S(2)}, u32[]{:S(2)}) %all-to-all-start) | async-done | bytes 524320 | tf_op jit(solution)/shard_map/all_to_all | solution.py:30
  38.2 54.3 %all-gather.3.cloned.1.call-done = bf16[5376,1024]{1,0:T(8,128)(2,1)} async-done(((bf16[5376,256]{1,0:T(8,128)(2,1)}), bf16[5376,1024]{1,0:T(8,128)(2,1)}) %all-gather.3.cloned.1.call-update) | async-done | bytes 11010064 | tf_op jit(solution)/shard_map/all_gather | solution.py:33
  92.5 6.5 %fusion = f32[256,5376]{1,0:T(8,128)S(1)} fusion(bf16[256,1024]{0,1:T(8,128)(2,1)S(1)} %bitcast.11, bf16[5376,1024]{1,0:T(8,128)(2,1)} %all-gather.3.cloned.1.call-done, f32[256]{0:T(256)S(1)} %dynamic_slice.11, f32[256]{0:T(256)S(1)} %dynamic_slice.10), kind=kOutput, calls=%fused_computation.7 | convolution fusion | flops 2821324800 | bytes 17041408 | tf_op jit(solution)/shard_map/dot_general | solution.py:31
  99.1 0.0 copy-start.1
  99.1 18.2 %fusion.12 = (bf16[256,5376]{1,0:T(8,128)(2,1)}, f32[]{:T(128)}) fusion(f32[256,5376]{1,0:T(8,128)S(1)} %fusion, f32[]{:T(128)S(6)} %div.31, f32[256]{0:T(256)S(1)} %dynamic_slice.11, s32[5376]{0:T(1024)S(1)} %iota_add_fusion, s32[256]{0:T(256)S(1)} %dynamic_slice.9, s32[2,5376]{1,0:T(2,128)S(1)} %copy-done.3, s32[256]{0:T(256)S(1)} %and_select_fusion), kind=kOutput, calls=%fused_computation.25 | convolution fusion | flops 94972928 | bytes 8325128 | tf_op jit(solution)/shard_map/dot_general | solution.py:44
  117.3 0.0 all-gather.5.cloned.1.call-update
  117.3 0.0 all-reduce.3.cloned.1.call-start
  117.4 40.5 %psum.43 = f32[]{:T(128)} all-reduce(f32[]{:T(128)} %get-tuple-element.12), channel_id=1, replica_groups=mesh['img'=2,'cls'=4,'emb'=4] {'img','cls','emb'}, use_global_device_ids=true, to_apply=%region_3.5 | all-reduce | flops 1 | bytes 8 | tf_op jit(solution)/shard_map/psum | solution.py:50
  159.2 32.3 %all-gather.5.cloned.1.call-done = bf16[1024,5376]{1,0:T(8,128)(2,1)} async-done(((bf16[256,5376]{1,0:T(8,128)(2,1)}), bf16[1024,5376]{1,0:T(8,128)(2,1)}) %all-gather.5.cloned.1.call-update) | async-done | bytes 11010064 | tf_op jit(solution)/shard_map/all_gather | solution.py:53
  191.5 8.1 %fusion.37 = f32[1024,256]{1,0:T(8,128)} fusion(bf16[1024,5376]{1,0:T(8,128)(2,1)} %all-gather.5.cloned.1.call-done, bf16[5376,256]{1,0:T(8,128)(2,1)S(1)} %copy-done.1), kind=kOutput, calls=%fused_computation.63 | convolution fusion | flops 2818572288 | bytes 14811136 | tf_op jit(solution)/shard_map/dot_general | solution.py:54
  199.6 0.0 all-reduce.3.cloned.1.call-update
  199.7 9.6 %fusion.38 = f32[5376,256]{1,0:T(8,128)} fusion(bf16[1024,5376]{1,0:T(8,128)(2,1)} %all-gather.5.cloned.1.call-done, bf16[1024,256]{1,0:T(8,128)(2,1)S(1)} %fusion.28), kind=kOutput, calls=%fused_computation.64 | convolution fusion | flops 2818572288 | bytes 17039360 | tf_op jit(solution)/shard_map/dot_general | solution.py:55
  209.2 131.1 %all-reduce.4 = bf16[5376,256]{1,0:T(8,128)(2,1)} all-reduce(f32[5376,256]{1,0:T(8,128)} %fusion.38), channel_id=1, replica_groups=mesh['img'=2,'cls'=4,'emb'=4] {'img'}, use_global_device_ids=true, to_apply=%region_9.11 | all-reduce | flops 1376256 | bytes 8257536 | tf_op jit(solution)/shard_map/psum | solution.py:61
  340.4 0.0 copy-done
  340.4 1.6 fusion.29
  342.0 5.9 %psum.46 = f32[1024]{0:T(1024)S(1)} all-reduce(f32[1024]{0:T(1024)S(1)} %fusion.29), channel_id=1, replica_groups=mesh['img'=2,'cls'=4,'emb'=4] {'emb'}, use_global_device_ids=true, to_apply=%region_8.10 | all-reduce | flops 1024 | bytes 8192 | tf_op jit(solution)/shard_map/psum | solution.py:59
  347.9 2.4 fusion.32
  (8 shorter events, 0.0 us)
Async XLA Ops:
  7.2 16.3 %copy-start.2 = (s32[1024]{0:T(1024)S(1)}, s32[1024]{0:T(1024)}, u32[]{:S(2)}) copy-start(s32[1024]{0:T(1024)} %param.11) | copy-start | bytes 12292
  7.2 85.4 %all-gather.3.cloned.1.call-start = ((), (), s32[]{:S(2)}) async-start(), calls=%async_computation.1 | async-start | bytes 13762560 | tf_op jit(solution)/shard_map/all_gather | solution.py:33
  19.9 18.4 %all-to-all-start = ((bf16[4,256,256]{1,2,0:T(8,128)(2,1)}), bf16[4,256,256]{1,2,0:T(8,128)(2,1)S(1)}, u32[]{:S(2)}, u32[]{:S(2)}) async-start(bf16[4,256,256]{1,2,0:T(8,128)(2,1)} %copy.9), calls=%async_computation | async-start | bytes 1048576 | tf_op jit(solution)/shard_map/all_to_all | solution.py:30
  23.4 168.1 %all-gather.5.cloned.1.call-start = ((), (), s32[]{:S(2)}) async-start(), calls=%async_computation.2 | async-start | bytes 13762560 | tf_op jit(solution)/shard_map/all_gather | solution.py:53
  92.5 6.5 %copy-start.3 = (s32[2,5376]{1,0:T(2,128)S(1)}, s32[2,5376]{1,0:T(2,128)}, u32[]{:S(2)}) copy-start(s32[2,5376]{1,0:T(2,128)} %param.12) | copy-start | bytes 129028
  99.1 92.4 %copy-start.1 = (bf16[5376,256]{1,0:T(8,128)(2,1)S(1)}, bf16[5376,256]{1,0:T(8,128)(2,1)}, u32[]{:S(2)}) copy-start(bf16[5376,256]{1,0:T(8,128)(2,1)} %param.8) | copy-start | bytes 8257540
  117.3 223.1 %all-reduce.3.cloned.1.call-start = ((), (), s32[]{:S(2)}) async-start(), calls=%async_computation.3 | async-start | bytes 2097152 | tf_op jit(solution)/shard_map/psum | solution.py:58
  209.2 131.2 %copy-start = (bf16[1024,256]{1,0:T(8,128)(2,1)S(1)}, bf16[1024,256]{1,0:T(8,128)(2,1)}, u32[]{:S(2)}) copy-start(bf16[1024,256]{1,0:T(8,128)(2,1)} %param.7) | copy-start | bytes 1572868
Sparse Core Ops, SparseCore 0:
  9.5 82.9 all-gather.2
  117.4 74.0 all-gather.4
  199.8 51.7 all-reduce.2
where the time goes:
time: 359 us; the launch traced here: 358 us
  blocking collectives  191 us (53%)
  waiting for transfers between devices  93.6 us (26%)
  matrix products  42.4 us (12%)
  between operations  17 us (5%)
  other arithmetic  7.16 us (2%)
  starting transfers between devices  3.66 us (1%)
    psum x1, blocking collectives, shards(): table_grad = lax.psum(table_acc, 'img').astype(jnp.bfloat16)  131 us
    all_gather x1, waiting for transfers between devices, shards(): lax.all_gather(table, 'emb', axis=1, tiled=True)  54.3 us
    psum x1, blocking collectives, shards(): total = lax.psum(jnp.sum(term * mask), ('img', 'cls', 'emb'))  40.5 us
    all_gather x1, waiting for transfers between devices, shards(): piece = lax.all_gather(dscore, 'emb', axis=0, tiled=True)  32.3 us
    dot_general x1, matrix products, shards(): jnp.dot(onehot, valid.astype(jnp.float32), preferred_element_type=jnp.flo...  18.2 us
    dot_general x1, matrix products, shards(): lax.dot_general(piece, unit_b, (((0,), (0,)), ((), ())), preferred_elemen...  9.56 us
    psum x1, blocking collectives, shards(): squares = lax.psum(jnp.sum(block * block, axis=1), 'emb')  8.38 us
    dot_general x1, matrix products, shards(): dunit_piece = jnp.dot(piece, table, preferred_element_type=jnp.float32)  8.13 us
  transfers between devices with their start and end apart: 4, of which 3 were waited for; matrix products, arithmetic and copies ran while one was open for 4% of the time, Pallas kernels for 0%

commit v1 on v0

--- a/solution.py
+++ b/solution.py
@@ -30,7 +30,7 @@
     unit_rows = lax.all_to_all(unit_b, "emb", split_axis=0, concat_axis=1, tiled=True)
     cosine = lax.dot_general(
         unit_rows,
-        lax.all_gather(table, "emb", axis=1, tiled=True),
+        jnp.concatenate(lax.all_gather(table, "emb"), axis=1),
         (((1,), (1,)), ((), ())),
         preferred_element_type=jnp.float32,
     )

time: 359 us -> 357 us (level)
  transfers between devices with their start and end apart: 4 -> 4, of which waited for: 3 -> 3; matrix products, arithmetic and copies ran while one was open for 4% -> 5% of each run, Pallas kernels for 0% -> 0%
where the time goes in v1:
time: 357 us; the launch traced here: 356 us
  blocking collectives  191 us (54%)
  waiting for transfers between devices  91.2 us (26%)
  matrix products  41.9 us (12%)
  between operations  16.9 us (5%)
  other arithmetic  8.66 us (2%)
  starting transfers between devices  3.61 us (1%)
    psum x1, blocking collectives, shards(): table_grad = lax.psum(table_acc, 'img').astype(jnp.bfloat16)  131 us
    all_gather x1, waiting for transfers between devices, shards(): lax.all_gather(table, 'emb')  53.1 us
    psum x1, blocking collectives, shards(): total = lax.psum(jnp.sum(term * mask), ('img', 'cls', 'emb'))  40.4 us
    all_gather x1, waiting for transfers between devices, shards(): piece = lax.all_gather(dscore, 'emb', axis=0, tiled=True)  32.5 us
    dot_general x1, matrix products, shards(): jnp.dot(onehot, valid.astype(jnp.float32), preferred_element_type=jnp.flo...  18.2 us
    dot_general x1, matrix products, shards(): lax.dot_general(piece, unit_b, (((0,), (0,)), ((), ())), preferred_elemen...  9.6 us
    psum x1, blocking collectives, shards(): squares = lax.psum(jnp.sum(block * block, axis=1), 'emb')  8.38 us
    dot_general x1, matrix products, shards(): dunit_piece = jnp.dot(piece, table, preferred_element_type=jnp.float32)  8.13 us
  transfers between devices with their start and end apart: 4, of which 3 were waited for; matrix products, arithmetic and copies ran while one was open for 5% of the time, Pallas kernels for 0%

profile of v1, /device:TPU:0, one launch (start us, length us, event | category | flops | bytes accessed | tf_op | source)
XLA Modules:
  0.0 355.9 jit_solution(14972819573240790919)
XLA Ops:
  7.2 0.0 all-gather.6.cloned.1.call-start
  7.2 0.7 all-gather.6.cloned.1.call-update
  7.9 1.3 fusion.34
  9.2 8.4 %psum.42 = f32[1024]{0:T(1024)S(1)} all-reduce(f32[1024]{0:T(1024)S(1)} %fusion.34), channel_id=1, replica_groups=mesh['img'=2,'cls'=4,'emb'=4] {'emb'}, use_global_device_ids=true, to_apply=%region_1.0 | all-reduce | flops 1024 | bytes 8192 | tf_op jit(solution)/shard_map/psum | solution.py:24
  17.5 2.1 fusion.29
  19.7 3.5 all-to-all-start
  23.2 0.0 all-gather.4.cloned.1.call-start
  23.2 1.3 convert_reduce_fusion
  24.5 5.5 %psum.44 = f32[]{:T(128)} all-reduce(f32[]{:T(128)} %convert_reduce_fusion), channel_id=1, replica_groups=mesh['img'=2,'cls'=4,'emb'=4] {'img'}, use_global_device_ids=true, to_apply=%region_5.7 | all-reduce | flops 1 | bytes 8 | tf_op jit(solution)/shard_map/psum | solution.py:26
  30.0 0.8 dynamic_slice.9
  30.8 0.8 dynamic_slice.11
  31.6 0.8 dynamic_slice.10
  33.0 4.9 %all-to-all-done = bf16[4,256,256]{2,1,0:T(8,128)(2,1)S(1)} async-done(((bf16[4,256,256]{2,1,0:T(8,128)(2,1)}), bf16[4,256,256]{2,1,0:T(8,128)(2,1)S(1)}, u32[]{:S(2)}, u32[]{:S(2)}) %all-to-all-start) | async-done | bytes 524320 | tf_op jit(solution)/shard_map/all_to_all | solution.py:30
  38.0 53.1 %all-gather.6.cloned.1.call-done = bf16[21504,256]{1,0:T(8,128)(2,1)} async-done(((bf16[5376,256]{1,0:T(8,128)(2,1)}), bf16[21504,256]{1,0:T(8,128)(2,1)}) %all-gather.6.cloned.1.call-update) | async-done | bytes 11010064 | tf_op jit(solution)/shard_map/all_gather | solution.py:33
  91.1 0.0 copy-start.2
  91.1 6.0 %fusion.1 = f32[256,5376]{1,0:T(8,128)S(1)} fusion(bf16[5376,4,256]{2,0,1:T(8,128)(2,1)} %bitcast.18, f32[256]{0:T(256)S(1)} %dynamic_slice.11, f32[256]{0:T(256)S(1)} %dynamic_slice.10, bf16[4,256,256]{2,1,0:T(8,128)(2,1)S(1)} %all-to-all-done), kind=kOutput, calls=%fused_computation.8 | convolution fusion | flops 2821324800 | bytes 17041408 | tf_op jit(solution)/shard_map/dot_general | solution.py:31
  97.0 0.0 copy-done.2
  97.1 0.0 copy-start.1
  97.1 18.2 %fusion.13 = (bf16[256,5376]{1,0:T(8,128)(2,1)}, f32[]{:T(128)}) fusion(f32[256,5376]{1,0:T(8,128)S(1)} %fusion.1, f32[]{:T(128)S(6)} %div.31, f32[256]{0:T(256)S(1)} %dynamic_slice.11, s32[5376]{0:T(1024)S(1)} %iota_add_fusion, s32[256]{0:T(256)S(1)} %dynamic_slice.9, s32[2,5376]{1,0:T(2,128)S(1)} %copy-done.2, s32[256]{0:T(256)S(1)} %and_select_fusion), kind=kOutput, calls=%fused_computation.26 | convolution fusion | flops 94972928 | bytes 8325128 | tf_op jit(solution)/shard_map/dot_general | solution.py:44
  115.2 0.0 all-gather.4.cloned.1.call-update
  115.3 0.0 all-reduce.3.cloned.1.call-start
  115.3 40.4 %psum.43 = f32[]{:T(128)} all-reduce(f32[]{:T(128)} %get-tuple-element.12), channel_id=1, replica_groups=mesh['img'=2,'cls'=4,'emb'=4] {'img','cls','emb'}, use_global_device_ids=true, to_apply=%region_3.5 | all-reduce | flops 1 | bytes 8 | tf_op jit(solution)/shard_map/psum | solution.py:50
  157.0 32.5 %all-gather.4.cloned.1.call-done = bf16[1024,5376]{1,0:T(8,128)(2,1)} async-done(((bf16[256,5376]{1,0:T(8,128)(2,1)}), bf16[1024,5376]{1,0:T(8,128)(2,1)}) %all-gather.4.cloned.1.call-update) | async-done | bytes 11010064 | tf_op jit(solution)/shard_map/all_gather | solution.py:53
  189.4 0.0 copy-done.1
  189.4 8.1 %fusion.39 = f32[1024,256]{1,0:T(8,128)} fusion(bf16[1024,5376]{1,0:T(8,128)(2,1)} %all-gather.4.cloned.1.call-done, bf16[5376,256]{1,0:T(8,128)(2,1)S(1)} %copy-done.1), kind=kOutput, calls=%fused_computation.65 | convolution fusion | flops 2818572288 | bytes 14811136 | tf_op jit(solution)/shard_map/dot_general | solution.py:54
  197.6 0.0 all-reduce.3.cloned.1.call-update
  197.6 9.6 %fusion.40 = f32[5376,256]{1,0:T(8,128)} fusion(bf16[1024,5376]{1,0:T(8,128)(2,1)} %all-gather.4.cloned.1.call-done, bf16[1024,256]{1,0:T(8,128)(2,1)} %fusion.29), kind=kOutput, calls=%fused_computation.66 | convolution fusion | flops 2818572288 | bytes 17039360 | tf_op jit(solution)/shard_map/dot_general | solution.py:55
  207.2 131.1 %all-reduce.4 = bf16[5376,256]{1,0:T(8,128)(2,1)} all-reduce(f32[5376,256]{1,0:T(8,128)} %fusion.40), channel_id=1, replica_groups=mesh['img'=2,'cls'=4,'emb'=4] {'img'}, use_global_device_ids=true, to_apply=%region_9.11 | all-reduce | flops 1376256 | bytes 8257536 | tf_op jit(solution)/shard_map/psum | solution.py:61
  338.4 0.0 copy-done
  338.4 1.6 fusion.30
  340.0 5.9 %psum.46 = f32[1024]{0:T(1024)S(1)} all-reduce(f32[1024]{0:T(1024)S(1)} %fusion.30), channel_id=1, replica_groups=mesh['img'=2,'cls'=4,'emb'=4] {'emb'}, use_global_device_ids=true, to_apply=%region_8.10 | all-reduce | flops 1024 | bytes 8192 | tf_op jit(solution)/shard_map/psum | solution.py:59
  345.9 2.4 fusion.33
  (5 shorter events, 0.0 us)
Async XLA Ops:
  7.2 83.9 %all-gather.6.cloned.1.call-start = ((), (), s32[]{:S(2)}) async-start(), calls=%async_computation.3 | async-start | bytes 13762560 | tf_op jit(solution)/shard_map/all_gather | solution.py:33
  19.7 18.3 %all-to-all-start = ((bf16[4,256,256]{2,1,0:T(8,128)(2,1)}), bf16[4,256,256]{2,1,0:T(8,128)(2,1)S(1)}, u32[]{:S(2)}, u32[]{:S(2)}) async-start(bf16[4,256,256]{2,1,0:T(8,128)(2,1)} %bitcast), calls=%async_computation | async-start | bytes 1048576 | tf_op jit(solution)/shard_map/all_to_all | solution.py:30
  23.2 166.3 %all-gather.4.cloned.1.call-start = ((), (), s32[]{:S(2)}) async-start(), calls=%async_computation.1 | async-start | bytes 13762560 | tf_op jit(solution)/shard_map/all_gather | solution.py:53
  91.1 6.0 %copy-start.2 = (s32[2,5376]{1,0:T(2,128)S(1)}, s32[2,5376]{1,0:T(2,128)}, u32[]{:S(2)}) copy-start(s32[2,5376]{1,0:T(2,128)} %param.12) | copy-start | bytes 129028
  97.1 92.4 %copy-start.1 = (bf16[5376,256]{1,0:T(8,128)(2,1)S(1)}, bf16[5376,256]{1,0:T(8,128)(2,1)}, u32[]{:S(2)}) copy-start(bf16[5376,256]{1,0:T(8,128)(2,1)} %param.8) | copy-start | bytes 8257540
  115.3 223.1 %all-reduce.3.cloned.1.call-start = ((), (), s32[]{:S(2)}) async-start(), calls=%async_computation.2 | async-start | bytes 2097152 | tf_op jit(solution)/shard_map/psum | solution.py:58
  207.2 131.2 %copy-start = (bf16[1024,256]{1,0:T(8,128)(2,1)S(1)}, bf16[1024,256]{1,0:T(8,128)(2,1)}, u32[]{:S(2)}) copy-start(bf16[1024,256]{1,0:T(8,128)(2,1)} %param.7) | copy-start | bytes 1572868
Sparse Core Ops, SparseCore 0:
  9.5 81.4 all-gather.5
  115.4 74.0 all-gather.3
  197.7 51.7 all-reduce.2
